TPU v7x, 256 devices: a whole 4x4x8 slice. The times are simulated.
256 devices in a mesh: gx: 8 (over x, core), gy: 4 (over y), gz: 8 (over z).
Axes of the slice: x: 4, y: 4, z: 8, core: 2. Of those that a mesh axis runs over, the one named last changes fastest.
Arguments:
- left_core: float32 [256, 4096, 256], P(None, ('gx', 'gy', 'gz')), may hold values from -4000 to 4000
- right_core: float32 [256, 4096, 256], P(None, ('gx', 'gy', 'gz')), may hold values from -0.00012207031 to 0.00012207031
Outputs:
- left_out: float32 [256, 4096, 128], P(None, ('gx', 'gy', 'gz'))
- right_out: float32 [128, 4096, 256], P(None, ('gx', 'gy', 'gz'))
- next_factor: float32 [256, 256], replicated
All inputs are finite; a program needn't handle non-finite values.
Results may differ from a plain program's by a relative error of at most 0.000075.
Values sent between devices are 32-bit elements; how exact they have to be, the bound alone decides.
A program may use at most 192 MiB of HBM per device.

v0:
```python
import math
import jax
import jax.numpy as jnp
from jax import lax
from jax.sharding import PartitionSpec as P

RK = 128


def gram_of(matrix_rows):
    return lax.dot_general(
        matrix_rows,
        matrix_rows,
        (((0,), (0,)), ((), ())),
        precision=lax.Precision.HIGHEST,
        preferred_element_type=jnp.float32,
    )


def per_device(left_core, right_core):
    rank_left, points_local, rank_mid = left_core.shape
    rank_right = right_core.shape[2]
    total_points = points_local * lax.axis_size("gx") * lax.axis_size("gy") * lax.axis_size("gz")
    unfold = left_core.reshape(rank_left * points_local, rank_mid)
    lower_one = jnp.linalg.cholesky(lax.psum(gram_of(unfold), ("gx", "gy", "gz")))
    upper_full = lower_one.T
    ortho_cols = lax.linalg.triangular_solve(
        lower_one[:RK, :RK], unfold[:, :RK], left_side=False, lower=True, transpose_a=True
    )
    left_out = (ortho_cols * math.sqrt(rank_left * total_points)).reshape(
        rank_left, points_local, RK
    )
    absorbed = jnp.dot(
        upper_full[:RK, :],
        right_core.reshape(rank_mid, points_local * rank_right),
        precision=lax.Precision.HIGHEST,
        preferred_element_type=jnp.float32,
    )
    summed = lax.psum(gram_of(absorbed.reshape(RK * points_local, rank_right)), ("gx", "gy", "gz"))
    factor = jnp.linalg.cholesky(summed / (RK * total_points)).T
    right_out = absorbed.reshape(RK, points_local, rank_right)
    return (left_out, right_out, factor)


def solution(mesh):
    in_specs = (P(None, ("gx", "gy", "gz"), None), P(None, ("gx", "gy", "gz"), None))
    out_specs = (P(None, ("gx", "gy", "gz"), None), P(None, ("gx", "gy", "gz"), None), P())
    return jax.shard_map(
        per_device, mesh=mesh, in_specs=in_specs, out_specs=out_specs, check_vma=False
    )
```

profile of v0, /device:TPU:2, one launch (start us, length us, event | category | flops | bytes accessed | tf_op | source)
XLA Modules:
  0.0 617.6 jit_solution(7845188268302011180)
XLA Ops:
  7.2 0.0 all-reduce.4.cloned.1.call-start
  7.2 10.9 %convolution_bitcast_fusion = f32[256,256]{0,1:T(8,128)} fusion(f32[256,16,256]{2,1,0:T(8,128)} %param.3), kind=kOutput, calls=%fused_computation.3 | convolution fusion | flops 3221225472 | bytes 4456448 | tf_op jit(solution)/shard_map/dot_general | solution.py:11
  18.1 0.0 all-reduce.4.cloned.1.call-update
  18.1 0.5 all-reduce.6.cloned.1.call-start
  18.6 7.9 %copy.26 = f32[32,8,16,256]{3,1,2,0:T(8,128)} copy(f32[32,8,16,256]{3,2,1,0:T(8,128)} %bitcast.53) | data formatting | bytes 8388608
  26.5 244.9 %all-reduce.4.cloned.1.call-done = f32[256,256]{0,1:T(8,128)} async-done(((f32[256,256]{0,1:T(8,128)}), f32[256,256]{0,1:T(8,128)}) %all-reduce.4.cloned.1.call-update) | async-done | bytes 262160 | tf_op jit(solution)/shard_map/psum | solution.py:25
  271.5 1.1 copy.16
  272.6 1.0 fusion.3
  273.6 11.7 %cholesky.130 = f32[128,128]{1,0:T(8,128)S(1)} custom-call(f32[128,128]{1,0:T(8,128)S(1)} %cholesky.194), custom_call_target="Cholesky" | custom-call | tf_op jit(solution)/shard_map/jit(cholesky)/cholesky | solution.py:25
  285.3 9.8 %custom-call.13 = f32[1,128,128]{1,2,0:T(8,128)S(1)} custom-call(f32[1,128,128]{2,1,0:T(8,128)S(1)} %get-tuple-element.17), custom_call_target="InvertDiagBlocksLowerTriangular" | custom-call | tf_op jit(solution)/shard_map/jit(cholesky)/cholesky | solution.py:25
  295.2 0.2 constant_dynamic-update-slice_fusion.3
  295.4 0.3 convolution_subtract_fusion.1
  295.6 11.9 %cholesky.147 = f32[128,128]{1,0:T(8,128)S(1)} custom-call(f32[128,128]{1,0:T(8,128)S(1)} %convolution_subtract_fusion.1), custom_call_target="Cholesky" | custom-call | tf_op jit(solution)/shard_map/jit(cholesky)/cholesky | solution.py:25
  307.5 0.6 compare_reduce_fusion.2
  309.6 4.5 fusion.4
  314.1 1.5 reshape.39
  315.5 6.4 %fusion.14 = f32[256,256]{0,1:T(8,128)} fusion(f32[2048,256]{1,0:T(8,128)} %reshape.39), kind=kOutput, calls=%fused_computation.41 | convolution fusion | flops 1610612736 | bytes 2359296 | tf_op jit(solution)/shard_map/dot_general | solution.py:11
  321.9 0.0 all-reduce.6.cloned.1.call-update
  322.0 9.8 %custom-call.11 = f32[1,128,128]{1,2,0:T(8,128)S(1)} custom-call(f32[1,128,128]{2,1,0:T(8,128)S(1)} %fusion.8), custom_call_target="InvertDiagBlocksLowerTriangular" | custom-call | tf_op jit(solution)/shard_map/triangular_solve | solution.py:27
  331.8 4.9 fusion
  336.7 2.0 copy.27
  338.6 3.1 copy.17
  341.7 229.4 %all-reduce.6.cloned.1.call-done = f32[256,256]{0,1:T(8,128)} async-done(((f32[256,256]{0,1:T(8,128)}), f32[256,256]{0,1:T(8,128)}) %all-reduce.6.cloned.1.call-update) | async-done | bytes 262160 | tf_op jit(solution)/shard_map/psum | solution.py:39
  571.1 1.0 broadcast_multiply_fusion
  572.0 0.1 copy.19
  572.2 1.0 fusion.2
  573.2 11.7 %cholesky.164 = f32[128,128]{1,0:T(8,128)S(1)} custom-call(f32[128,128]{1,0:T(8,128)S(1)} %cholesky.197), custom_call_target="Cholesky" | custom-call | tf_op jit(solution)/shard_map/jit(cholesky)/cholesky | solution.py:40
  585.0 9.8 %custom-call.14 = f32[1,128,128]{1,2,0:T(8,128)S(1)} custom-call(f32[1,128,128]{2,1,0:T(8,128)S(1)} %get-tuple-element.13), custom_call_target="InvertDiagBlocksLowerTriangular" | custom-call | tf_op jit(solution)/shard_map/jit(cholesky)/cholesky | solution.py:40
  594.8 0.2 constant_dynamic-update-slice_fusion.1
  595.0 0.3 convolution_subtract_fusion
  595.3 11.7 %cholesky.181 = f32[128,128]{1,0:T(8,128)S(1)} custom-call(f32[128,128]{1,0:T(8,128)S(1)} %convolution_subtract_fusion), custom_call_target="Cholesky" | custom-call | tf_op jit(solution)/shard_map/jit(cholesky)/cholesky | solution.py:40
  607.0 0.7 compare_reduce_fusion
  607.7 0.6 compare_reduce_fusion.1
  609.7 0.8 copy.20
  (12 shorter events, 0.3 us)
Async XLA Ops:
  7.2 264.3 %all-reduce.4.cloned.1.call-start = ((), (), s32[]{:S(2)}) async-start(), calls=%async_computation | async-start | bytes 524288 | tf_op jit(solution)/shard_map/psum | solution.py:25
  18.1 552.9 %all-reduce.6.cloned.1.call-start = ((), (), s32[]{:S(2)}) async-start(), calls=%async_computation.1 | async-start | bytes 524288 | tf_op jit(solution)/shard_map/psum | solution.py:39
Sparse Core Ops, SparseCore 0:
  18.2 253.1 all-reduce.3
  322.1 248.9 all-reduce.5
where the time goes:
time: 623 us; the launch traced here: 618 us
  waiting for transfers between devices  474 us (76%)
  other arithmetic  81.6 us (13%)
  matrix products  27.6 us (4%)
  between operations  17.1 us (3%)
  local copies, waits for them, and re-layouts  16.5 us (3%)
    psum x1, waiting for transfers between devices, per_device(): lax.psum(gram_of(unfold), ('gx', 'gy', 'gz'))  245 us
    psum x1, waiting for transfers between devices, per_device(): lax.psum(gram_of(absorbed.reshape(RK * points_local, rank_right)), ('gx',...  229 us
    another operation x7, other arithmetic, per_device(): factor = jnp.linalg.cholesky(summed / (RK * total_points)).T  34.7 us
    another operation x6, other arithmetic, per_device(): jnp.linalg.cholesky(lax.psum(gram_of(unfold), ('gx', 'gy', 'gz')))  34.1 us
    dot_general x2, matrix products, gram_of(): lax.dot_general(matrix_rows, matrix_rows, (((0,), (0,)), ((), ())), preci...  17.3 us
  transfers between devices with their start and end apart: 2, of which 2 were waited for; matrix products, arithmetic and copies ran while one was open for 4% of the time, Pallas kernels for 0%

commit v1 on v0

--- a/solution.py
+++ b/solution.py
@@ -36,7 +36,8 @@
         precision=lax.Precision.HIGHEST,
         preferred_element_type=jnp.float32,
     )
-    summed = lax.psum(gram_of(absorbed.reshape(RK * points_local, rank_right)), ("gx", "gy", "gz"))
+    inner = lax.psum(gram_of(absorbed.reshape(RK * points_local, rank_right)), ("gy", "gz"))
+    summed = lax.psum(inner, "gx")
     factor = jnp.linalg.cholesky(summed / (RK * total_points)).T
     right_out = absorbed.reshape(RK, points_local, rank_right)
     return (left_out, right_out, factor)

time: 623 us -> 581 us (0.933)
  waiting for transfers between devices: 474 us -> 430 us
    psum x1 -> x2, waiting for transfers between devices: 229 us -> 185 us  [the longest x1 133 us: per_device(): lax.psum(gram_of(absorbed.reshape(RK * points_local, rank_right)), ('gy',...]
  transfers between devices with their start and end apart: 2 -> 3, of which waited for: 2 -> 3; matrix products, arithmetic and copies ran while one was open for 4% -> 5% of each run, Pallas kernels for 0% -> 0%
where the time goes in v1:
time: 581 us; the launch traced here: 573 us
  waiting for transfers between devices  430 us (74%)
  other arithmetic  81.6 us (14%)
  matrix products  27.6 us (5%)
  between operations  16.8 us (3%)
  local copies, waits for them, and re-layouts  16.5 us (3%)
    psum x1, waiting for transfers between devices, per_device(): lax.psum(gram_of(unfold), ('gx', 'gy', 'gz'))  245 us
    psum x1, waiting for transfers between devices, per_device(): lax.psum(gram_of(absorbed.reshape(RK * points_local, rank_right)), ('gy',...  133 us
    psum x1, waiting for transfers between devices, per_device(): summed = lax.psum(inner, 'gx')  52.1 us
    another operation x7, other arithmetic, per_device(): factor = jnp.linalg.cholesky(summed / (RK * total_points)).T  34.7 us
    another operation x6, other arithmetic, per_device(): jnp.linalg.cholesky(lax.psum(gram_of(unfold), ('gx', 'gy', 'gz')))  34.1 us
    dot_general x2, matrix products, gram_of(): lax.dot_general(matrix_rows, matrix_rows, (((0,), (0,)), ((), ())), preci...  17.3 us
  transfers between devices with their start and end apart: 3, of which 3 were waited for; matrix products, arithmetic and copies ran while one was open for 5% of the time, Pallas kernels for 0%

profile of v1, /device:TPU:2, one launch (start us, length us, event | category | flops | bytes accessed | tf_op | source)
XLA Modules:
  0.0 573.3 jit_solution(3086018832396310289)
XLA Ops:
  7.2 0.0 all-reduce.5.cloned.1.call-start
  7.2 10.9 %convolution_bitcast_fusion = f32[256,256]{0,1:T(8,128)} fusion(f32[256,16,256]{2,1,0:T(8,128)} %param.3), kind=kOutput, calls=%fused_computation.3 | convolution fusion | flops 3221225472 | bytes 4456448 | tf_op jit(solution)/shard_map/dot_general | solution.py:11
  18.1 0.0 all-reduce.5.cloned.1.call-update
  18.1 0.5 all-reduce.7.cloned.1.call-start
  18.6 7.9 %copy.26 = f32[32,8,16,256]{3,1,2,0:T(8,128)} copy(f32[32,8,16,256]{3,2,1,0:T(8,128)} %bitcast.53) | data formatting | bytes 8388608
  26.5 244.9 %all-reduce.5.cloned.1.call-done = f32[256,256]{0,1:T(8,128)} async-done(((f32[256,256]{0,1:T(8,128)}), f32[256,256]{0,1:T(8,128)}) %all-reduce.5.cloned.1.call-update) | async-done | bytes 262160 | tf_op jit(solution)/shard_map/psum | solution.py:25
  271.5 1.1 copy.16
  272.6 1.0 fusion.3
  273.6 11.7 %cholesky.130 = f32[128,128]{1,0:T(8,128)S(1)} custom-call(f32[128,128]{1,0:T(8,128)S(1)} %cholesky.194), custom_call_target="Cholesky" | custom-call | tf_op jit(solution)/shard_map/jit(cholesky)/cholesky | solution.py:25
  285.3 9.8 %custom-call.13 = f32[1,128,128]{1,2,0:T(8,128)S(1)} custom-call(f32[1,128,128]{2,1,0:T(8,128)S(1)} %get-tuple-element.17), custom_call_target="InvertDiagBlocksLowerTriangular" | custom-call | tf_op jit(solution)/shard_map/jit(cholesky)/cholesky | solution.py:25
  295.2 0.2 constant_dynamic-update-slice_fusion.3
  295.4 0.3 convolution_subtract_fusion.1
  295.6 11.9 %cholesky.147 = f32[128,128]{1,0:T(8,128)S(1)} custom-call(f32[128,128]{1,0:T(8,128)S(1)} %convolution_subtract_fusion.1), custom_call_target="Cholesky" | custom-call | tf_op jit(solution)/shard_map/jit(cholesky)/cholesky | solution.py:25
  307.5 0.6 compare_reduce_fusion.2
  309.5 4.5 fusion.4
  314.0 1.5 reshape.39
  315.5 6.4 %fusion.14 = f32[256,256]{0,1:T(8,128)} fusion(f32[2048,256]{1,0:T(8,128)} %reshape.39), kind=kOutput, calls=%fused_computation.41 | convolution fusion | flops 1610612736 | bytes 2359296 | tf_op jit(solution)/shard_map/dot_general | solution.py:11
  321.9 0.0 all-reduce.7.cloned.1.call-update
  321.9 0.0 all-reduce.9.cloned.1.call-start
  322.0 9.8 %custom-call.11 = f32[1,128,128]{1,2,0:T(8,128)S(1)} custom-call(f32[1,128,128]{2,1,0:T(8,128)S(1)} %fusion.8), custom_call_target="InvertDiagBlocksLowerTriangular" | custom-call | tf_op jit(solution)/shard_map/triangular_solve | solution.py:27
  331.8 133.2 %all-reduce.7.cloned.1.call-done = f32[256,256]{0,1:T(8,128)} async-done(((f32[256,256]{0,1:T(8,128)}), f32[256,256]{0,1:T(8,128)}) %all-reduce.7.cloned.1.call-update) | async-done | bytes 262160 | tf_op jit(solution)/shard_map/psum | solution.py:39
  465.0 0.0 all-reduce.9.cloned.1.call-update
  465.0 4.9 fusion
  469.9 2.0 copy.27
  471.9 3.1 copy.17
  474.9 52.1 %all-reduce.9.cloned.1.call-done = f32[256,256]{0,1:T(8,128)} async-done(((f32[256,256]{0,1:T(8,128)}), f32[256,256]{0,1:T(8,128)}) %all-reduce.9.cloned.1.call-update) | async-done | bytes 262160 | tf_op jit(solution)/shard_map/psum | solution.py:40
  527.0 1.0 broadcast_multiply_fusion
  528.0 0.1 copy.19
  528.1 1.0 fusion.2
  529.1 11.7 %cholesky.164 = f32[128,128]{1,0:T(8,128)S(1)} custom-call(f32[128,128]{1,0:T(8,128)S(1)} %cholesky.197), custom_call_target="Cholesky" | custom-call | tf_op jit(solution)/shard_map/jit(cholesky)/cholesky | solution.py:41
  540.9 9.8 %custom-call.14 = f32[1,128,128]{1,2,0:T(8,128)S(1)} custom-call(f32[1,128,128]{2,1,0:T(8,128)S(1)} %get-tuple-element.13), custom_call_target="InvertDiagBlocksLowerTriangular" | custom-call | tf_op jit(solution)/shard_map/jit(cholesky)/cholesky | solution.py:41
  550.7 0.2 constant_dynamic-update-slice_fusion.1
  550.9 0.3 convolution_subtract_fusion
  551.2 11.7 %cholesky.181 = f32[128,128]{1,0:T(8,128)S(1)} custom-call(f32[128,128]{1,0:T(8,128)S(1)} %convolution_subtract_fusion), custom_call_target="Cholesky" | custom-call | tf_op jit(solution)/shard_map/jit(cholesky)/cholesky | solution.py:41
  563.0 0.7 compare_reduce_fusion
  563.7 0.6 compare_reduce_fusion.1
  565.7 0.8 copy.20
  (12 shorter events, 0.3 us)
Async XLA Ops:
  7.2 264.3 %all-reduce.5.cloned.1.call-start = ((), (), s32[]{:S(2)}) async-start(), calls=%async_computation | async-start | bytes 524288 | tf_op jit(solution)/shard_map/psum | solution.py:25
  18.1 446.9 %all-reduce.7.cloned.1.call-start = ((), (), s32[]{:S(2)}) async-start(), calls=%async_computation.1 | async-start | bytes 524288 | tf_op jit(solution)/shard_map/psum | solution.py:39
  321.9 205.1 %all-reduce.9.cloned.1.call-start = ((), (), s32[]{:S(2)}) async-start(), calls=%async_computation.2 | async-start | bytes 524288 | tf_op jit(solution)/shard_map/psum | solution.py:40
Sparse Core Ops, SparseCore 0:
  18.2 253.1 all-reduce.4
  322.0 142.9 all-reduce.6
  467.3 59.6 all-reduce.8
